TPU v7x, 32 devices: a whole 2x2x4 slice. The times are simulated.
32 devices in a mesh: inst: 4 (over z), sector: 4 (over y, core), slab: 2 (over x).
Axes of the slice: x: 2, y: 2, z: 4, core: 2. Of those that a mesh axis runs over, the one named last changes fastest.
Arguments:
- adjoint_state: float32 [4, 4, 64, 8192], P('inst', None, None, ('sector', 'slab')), may hold values from -6 to 6
- mean_flow: float32 [3, 8192], P(None, ('sector', 'slab')), may hold values from -0.5 to 0.5
- metric: float32 [3, 8192], P(None, ('sector', 'slab')), may hold values from 0.5 to 2
- connectivity: int32 [6, 8192], P(None, ('sector', 'slab')), may hold values from 0 to 1279, as said below
- wall_flags: int32 [6, 8192], P(None, ('sector', 'slab')), may hold values 0 or 1
- donor_face_positions: int32 [4, 2048], P('inst', ('sector', 'slab')), may hold values from 0 to 510, as said below
- interp_weight: float32 [4], P('inst'), may hold values from 0 to 1
Outputs:
- residual: float32 [4, 4, 64, 8192], P('inst', None, None, ('sector', 'slab'))
- new_state: float32 [4, 4, 64, 8192], P('inst', None, None, ('sector', 'slab'))
Inputs may be any that keep to these rules, and one draw needn't show every extreme that they name: `connectivity`: within each block of 1024 columns: faces 0 to 3, face 4 of elements 256 and above and face 5 of elements below 768 name a local element below 1024; face 4 of the first 256 elements and face 5 of the last 256 elements name 1024 plus a distinct row of the neighbouring slab's layer. `donor_face_positions`: in each block of 256 columns, entry i of row t is i plus a rotation of instance t that is the same in every block.
All inputs are finite; a program needn't handle non-finite values. No bound on the sum of `wall_flags` on one device may be relied on, other than what follows from the above.
Results may differ from a plain program's by a relative error of at most 0.0003.
Values sent between devices are 32-bit elements; how exact they have to be, the bound alone decides.
No kernel may reach another device: no remote copies, remote signals or barrier semaphores. Data moves between devices by JAX's collectives and lax.ppermute only.
A program may use at most 192 MiB of HBM per device.

v0:
```python
import math
import jax
import jax.numpy as jnp
import numpy as np
from jax import lax
from jax.sharding import PartitionSpec as P

omega_scale = 0.5
nyquist_damping = 0.5
wave_bound = 1.5
pseudo_step = 0.05
maximum_harmonic = lax.Precision.HIGHEST


def padded_2(value, sides, width):
    for axis, dim in sides:
        size, length = (lax.axis_size(axis), value.shape[dim])
        up = [(i, (i + 1) % size) for i in range(size - 1)]
        down = [(j, i) for i, j in up]
        last = lax.slice_in_dim(value, length - width, length, axis=dim)
        leading = lax.slice_in_dim(value, 0, width, axis=dim)
        before = lax.ppermute(last, axis, up)
        after = lax.ppermute(leading, axis, down)
        value = jnp.concatenate([before, value, after], axis=dim)
    return value


def passed_along(value, axis, by):
    length = lax.axis_size(axis)
    return lax.ppermute(value, axis, [(i, (i + by) % length) for i in range(length)])


def derivative_tables():
    points = np.array([-1.0, -1.0 / math.sqrt(5.0), 1.0 / math.sqrt(5.0), 1.0])
    weights = np.array(
        [1.0 / np.prod([points[i] - points[m] for m in range(4) if m != i]) for i in range(4)]
    )
    matrix = np.zeros((4, 4))
    for i in range(4):
        for j in range(4):
            if i != j:
                matrix[i, j] = weights[j] / weights[i] / (points[i] - points[j])
        matrix[i, i] = -np.sum(matrix[i])
    identity = np.eye(4)
    return np.stack(
        [
            np.kron(np.kron(matrix, identity), identity),
            np.kron(np.kron(identity, matrix), identity),
            np.kron(np.kron(identity, identity), matrix),
        ]
    )


def selection_table():
    selector_matrix = np.zeros((96, 64))
    for f in range(6):
        k = f // 2
        layer_pos = 0 if f % 2 == 0 else 3
        for first in range(4):
            for second in range(4):
                indices = [first, second]
                indices.insert(k, layer_pos)
                selector_matrix[
                    16 * f + 4 * first + second, 16 * indices[0] + 4 * indices[1] + indices[2]
                ] = 1.0
    return selector_matrix


def spectral_matrix(count):
    row_index = jnp.arange(count, dtype=jnp.int32)[:, None]
    col_index = jnp.arange(count, dtype=jnp.int32)[None, :]
    offset = row_index - col_index
    parity = (1 - 2 * (offset % 2)).astype(jnp.float32)
    phase_angle = math.pi / count * offset.astype(jnp.float32)
    off_diag = offset != 0
    sine_val = jnp.where(off_diag, jnp.sin(phase_angle), 1.0)
    time_deriv = jnp.where(off_diag, 0.5 * parity * jnp.cos(phase_angle) / sine_val, 0.0)
    return -omega_scale * time_deriv - nyquist_damping / count * parity


def lookup_columns(lookup_table, columns):
    length = lookup_table.shape[2]
    indicator_matrix = (jnp.arange(length, dtype=jnp.int32)[:, None] == columns[None, :]).astype(
        jnp.float32
    )
    return jnp.einsum("xiz,zy->xiy", lookup_table, indicator_matrix, precision=maximum_harmonic)


def body_residual(
    state_of_block,
    spectral_term,
    differentiation_tables,
    selector_matrix,
    traces,
    mean_flow,
    metric,
    connectivity,
    wall_flags,
    ghost_low,
    ghost_high,
    iface_next,
    donor_positions,
    weight_value,
):
    variables = state_of_block.shape[0]
    elements = state_of_block.shape[2]
    iface_count = iface_next.shape[2]
    pseudo_gradient = (
        jnp.einsum(
            "fga,cat->fcgt", differentiation_tables, state_of_block, precision=maximum_harmonic
        )
        * metric[:, None, None, :]
    )
    advection = jnp.sum(mean_flow[:, None, None, :] * pseudo_gradient, axis=0)
    coupling = jnp.stack(
        [
            pseudo_gradient[0, 1] + pseudo_gradient[1, 2] + pseudo_gradient[2, 3],
            pseudo_gradient[0, 0],
            pseudo_gradient[1, 0],
            pseudo_gradient[2, 0],
        ]
    )
    residual = advection + coupling + spectral_term
    tables = [
        traces[0],
        traces[1],
        traces[2],
        traces[3],
        jnp.concatenate([traces[4], ghost_high], axis=2),
        jnp.concatenate([traces[5], ghost_low], axis=2),
    ]
    lifted_faces = []
    for f in range(6):
        k = f // 2
        orient = -1.0 if f % 2 == 0 else 1.0
        own_trace = traces[f]
        neighbour = lookup_columns(tables[f ^ 1], connectivity[f])
        mirror_sign = jnp.ones((variables,), jnp.float32).at[1 + k].set(-1.0)
        mirrored = own_trace * mirror_sign[:, None, None]
        neighbour = jnp.where(wall_flags[f][None, None, :] == 1, mirrored, neighbour)
        if f == 1:
            interface_rows = jnp.concatenate(
                [own_trace[:, :, elements - iface_count :], iface_next], axis=2
            )
            row_ids = jnp.arange(2 * iface_count, dtype=jnp.int32)[:, None]
            mixing_weight_matrix = (1.0 - weight_value) * (
                row_ids == donor_positions[None, :]
            ).astype(jnp.float32) + weight_value * (row_ids == donor_positions[None, :] + 1).astype(
                jnp.float32
            )
            blended = jnp.einsum(
                "xiz,zy->xiy", interface_rows, mixing_weight_matrix, precision=maximum_harmonic
            )
            neighbour = jnp.concatenate(
                [neighbour[:, :, : elements - iface_count], blended], axis=2
            )
        face_jump = neighbour - own_trace
        flux_jump = orient * mean_flow[k][None, None, :] * face_jump
        zero_row = jnp.zeros_like(face_jump[0])
        cross_terms = []
        for v in range(4):
            if v == 0:
                cross_terms.append(orient * face_jump[1 + k])
            elif v == 1 + k:
                cross_terms.append(orient * face_jump[0])
            else:
                cross_terms.append(zero_row)
        flux_jump = flux_jump + jnp.stack(cross_terms)
        lifted_faces.append(3.0 * metric[k][None, None, :] * (flux_jump + wave_bound * face_jump))
    lifted_everything = jnp.concatenate(lifted_faces, axis=1)
    return residual + jnp.einsum(
        "bc,sbh->sch", selector_matrix, lifted_everything, precision=maximum_harmonic
    )


def per_device(
    adjoint_state, mean_flow, metric, connectivity, wall_flags, donor_face_positions, interp_weight
):
    state_of_block = adjoint_state[0]
    variables, node_count, elements = state_of_block.shape
    rim_width = elements // 4
    iface_count = donor_face_positions.shape[1]
    differentiation_tables = jnp.asarray(derivative_tables(), jnp.float32)
    selector_matrix = jnp.asarray(selection_table(), jnp.float32)
    every_trace_set = jnp.einsum(
        "qa,yas->yqs", selector_matrix, state_of_block, precision=maximum_harmonic
    )
    traces = [every_trace_set[:, 16 * f : 16 * f + 16, :] for f in range(6)]
    slab_edge_rows = jnp.concatenate(
        [traces[4][:, :, :rim_width], traces[5][:, :, elements - rim_width :]], axis=2
    )
    padded = padded_2(slab_edge_rows, (("slab", 2),), rim_width)
    ghost_low = padded[:, :, :rim_width]
    ghost_high = padded[:, :, 3 * rim_width :]
    iface_next = passed_along(traces[1][:, :, elements - iface_count :], "sector", -1)
    spectral = spectral_matrix(lax.axis_size("inst"))
    flat_state = state_of_block.reshape(1, variables, node_count * elements)
    inst_row = lax.dynamic_index_in_dim(spectral, lax.axis_index("inst"), 0, keepdims=False)
    spectral_flat = jnp.einsum(
        "j,jvc->vc",
        inst_row,
        lax.all_gather(flat_state, "inst", axis=0, tiled=True),
        precision=maximum_harmonic,
    )
    spectral_term = spectral_flat.reshape(variables, node_count, elements)
    residual = body_residual(
        state_of_block,
        spectral_term,
        differentiation_tables,
        selector_matrix,
        traces,
        mean_flow,
        metric,
        connectivity,
        wall_flags,
        ghost_low,
        ghost_high,
        iface_next,
        donor_face_positions[0],
        interp_weight[0],
    )
    return (residual[None], (state_of_block + pseudo_step * residual)[None])


def solution(mesh):
    return jax.shard_map(
        per_device,
        mesh=mesh,
        in_specs=(
            P("inst", None, None, ("sector", "slab")),
            P(None, ("sector", "slab")),
            P(None, ("sector", "slab")),
            P(None, ("sector", "slab")),
            P(None, ("sector", "slab")),
            P("inst", ("sector", "slab")),
            P("inst"),
        ),
        out_specs=(
            P("inst", None, None, ("sector", "slab")),
            P("inst", None, None, ("sector", "slab")),
        ),
        check_vma=False,
    )
```

profile of v0, /device:TPU:0, one launch (start us, length us, event | category | flops | bytes accessed | tf_op | source)
XLA Modules:
  0.0 124.0 jit_solution(17806464936114319551)
XLA Ops:
  7.2 0.0 copy-start.4
  7.2 0.0 copy-start
  7.2 0.0 all-gather.2.cloned.1.call-start
  7.2 3.0 %reshape_squeeze.3 = f32[1,4,65536]{2,1,0:T(4,128)} reshape(f32[1,4,64,1024]{3,2,1,0:T(8,128)} %param.21) | data formatting | bytes 2097152 | tf_op jit(solution)/shard_map/reshape;squeeze | solution.py:197
  10.2 0.0 all-gather.2.cloned.1.call-update
  10.2 0.0 copy-done.4
  10.3 0.0 copy-done
  10.3 0.0 copy-start.9
  10.3 0.0 copy-start.6
  10.3 0.0 copy-start.10
  10.3 0.0 copy-start.7
  10.3 0.0 copy-start.8
  10.3 0.0 copy-start.13
  10.3 1.4 %convolution_bitcast_fusion = f32[4,96,1024]{2,1,0:T(8,128)S(1)} fusion(f32[96,64,1]{0,1,2:T(8,128)S(1)} %copy-done.4, f32[1,4,64,1024]{3,2,1,0:T(8,128)S(1)} %copy-done), kind=kOutput, calls=%fused_computation.28 | convolution fusion | flops 301989888 | bytes 2646016 | tf_op jit(solution)/shard_map/qa,yas->yqs/dot_general | solution.py:185
  11.8 0.7 fusion.126
  12.4 1.3 %collective-permute-start.2 = (f32[4,16,256]{2,1,0:T(8,128)S(1)}, f32[4,16,256]{2,1,0:T(8,128)}, u32[]{:S(2)}, u32[]{:S(2)}) collective-permute-start(f32[4,16,256]{2,1,0:T(8,128)S(1)} %get-tuple-element.75), channel_id=1, source_target_pairs={{1,0},{3,2},{5,4},{7,6},{9,8},{11,10},{13,12},{15,14},{17,16},{19,... | collective-permute-start | bytes 196616 | tf_op jit(solution)/shard_map/ppermute | solution.py:23
  13.7 6.1 %collective-permute-start.1 = (f32[4,16,256]{2,1,0:T(8,128)}, f32[4,16,256]{2,1,0:T(8,128)}, u32[]{:S(2)}, u32[]{:S(2)}) collective-permute-start(f32[4,16,256]{2,1,0:T(8,128)} %get-tuple-element.76), channel_id=1, source_target_pairs={{0,1},{2,3},{4,5},{6,7},{8,9},{10,11},{12,13},{14,15},{16,17},{18,... | collective-permute-start | bytes 196616 | tf_op jit(solution)/shard_map/ppermute | solution.py:22
  19.8 1.5 %collective-permute-start = (f32[4,16,256]{2,1,0:T(8,128)}, f32[4,16,256]{2,1,0:T(8,128)}, u32[]{:S(2)}, u32[]{:S(2)}) collective-permute-start(f32[4,16,256]{2,1,0:T(8,128)} %get-tuple-element.77), channel_id=1, source_target_pairs={{0,6},{2,0},{4,2},{6,4},{1,7},{3,1},{5,3},{7,5},{8,14},{10,8},{12,... | collective-permute-start | bytes 196616 | tf_op jit(solution)/shard_map/ppermute | solution.py:30
  22.0 0.0 copy-done.9
  22.1 0.1 compare_reduce_fusion
  22.1 0.0 copy-done.6
  22.2 0.0 copy-done.10
  22.2 0.0 copy-done.7
  22.3 0.0 copy-done.8
  22.3 0.0 copy-done.13
  22.3 1.7 %fusion.36 = f32[4,16,1024]{2,1,0:T(8,128)S(1)} fusion(s32[1024]{0:T(1024)S(1)} %bitcast.131, f32[4,96,1024]{2,1,0:T(8,128)S(1)} %convolution_bitcast_fusion, f32[4]{0:T(128)S(1)} %copy-done.13, pred[1024]{0:T(1024)(128)(4,1)S(1)} %get-tuple-element.64), kind=kOutput, calls=%fused_computation.34 | convolution fusion | flops 806551552 | bytes 792064 | tf_op jit(solution)/shard_map/xiz,zy->xiy/dot_general | solution.py:86
  24.0 0.0 copy-start.11
  24.0 1.7 %fusion.42 = f32[4,16,1024]{2,1,0:T(8,128)S(1)} fusion(s32[1024]{0:T(1024)S(1)} %bitcast.130, f32[4,96,1024]{2,1,0:T(8,128)S(1)} %convolution_bitcast_fusion, f32[4]{0:T(128)S(1)} %copy-done.13, pred[1024]{0:T(1024)(128)(4,1)S(1)} %get-tuple-element.63), kind=kOutput, calls=%fused_computation.36 | convolution fusion | flops 806551552 | bytes 792064 | tf_op jit(solution)/shard_map/xiz,zy->xiy/dot_general | solution.py:86
  25.7 0.0 copy-done.11
  25.7 1.6 %fusion.30 = f32[4,16,1024]{2,1,0:T(8,128)S(1)} fusion(s32[1024]{0:T(1024)S(1)} %bitcast.129, f32[4,96,1024]{2,1,0:T(8,128)S(1)} %convolution_bitcast_fusion, f32[4]{0:T(128)S(1)} %copy-done.11, pred[1024]{0:T(1024)(128)(4,1)S(1)} %get-tuple-element.66), kind=kOutput, calls=%fused_computation.32 | convolution fusion | flops 806551552 | bytes 792064 | tf_op jit(solution)/shard_map/xiz,zy->xiy/dot_general | solution.py:86
  27.4 0.0 copy-start.5
  27.4 1.6 %fusion.16 = f32[4,16,1024]{2,1,0:T(8,128)S(1)} fusion(s32[1024]{0:T(1024)S(1)} %bitcast.128, f32[4,96,1024]{2,1,0:T(8,128)S(1)} %convolution_bitcast_fusion), kind=kOutput, calls=%fused_computation.18 | convolution fusion | flops 806354944 | bytes 528384 | tf_op jit(solution)/shard_map/xiz,zy->xiy/dot_general | solution.py:86
  29.0 0.8 fusion.95
  29.8 0.1 slice_select_fusion
  29.9 0.0 copy-done.5
  29.9 3.7 %multiply_reduce_fusion = (f32[4,64,1024]{2,1,0:T(8,128)}, f32[3,4,64,1024]{3,2,1,0:T(8,128)S(1)}) fusion(f32[3,1024]{1,0:T(4,128)S(1)} %copy-done.6, f32[3,1024]{1,0:T(4,128)S(1)} %copy-done.7, f32[3,64,64,1]{2,1,3,0:T(8,128)S(1)} %copy-done.5, f32[1,4,64,1024]{3,2,1,0:T(8,128)S(1)} %copy-done), kind=kOutput, calls=%fused_computation.21 | convolution fusion | flops 606076928 | bytes 5316608 | tf_op jit(solution)/shard_map/fga,cat->fcgt/dot_general | solution.py:109
  33.6 0.8 fusion.100
  34.4 0.0 copy-start.12
  34.5 0.0 collective-permute-done
  34.5 1.4 %fusion.61 = f32[4,16,256]{2,1,0:T(8,128)S(1)} fusion(f32[]{:T(128)} %bitcast.110, s32[256]{0:T(256)S(1)} %bitcast.133, f32[]{:T(128)S(6)} %sub.46, s32[256]{0:T(256)S(1)} %bitcast.132, f32[4,16,256]{2,1,0:T(8,128)} %collective-permute-done, f32[4,16,256]{2,1,0:T(8,128)} %get-tuple-element.77), kind=kOutput, calls=%fused_computation.47 | convolution fusion | flops 101351424 | bytes 198664 | tf_op jit(solution)/shard_map/xiz,zy->xiy/dot_general | solution.py:151
  35.9 0.1 fusion.125
  36.0 0.0 collective-permute-done.1
  36.0 0.0 copy-done.12
  36.0 2.9 %fusion.48 = f32[4,16,1024]{2,1,0:T(8,128)S(1)} fusion(s32[1024]{0:T(1024)S(1)} %bitcast.127, f32[4,16,256]{2,1,0:T(8,128)} %collective-permute-done.1, f32[4,16,1024]{2,1,0:T(8,128)S(1)} %get-tuple-element.74, f32[4]{0:T(128)S(1)} %copy-done.12, pred[1024]{0:T(1024)(128)(4,1)S(1)} %get-tuple-element.67, f32[4,96,1024]{2,1,0:T(8,128)S(1)} %convolution_bitcast_fusion), kind=kOutput, calls=%fused_computation.38 | convolution fusion | flops 1008222208 | bytes 857104 | tf_op jit(solution)/shard_map/xiz,zy->xiy/dot_general | solution.py:86
  38.9 0.0 collective-permute-done.2
  38.9 3.1 %fusion.54 = f32[4,16,1024]{2,1,0:T(8,128)S(1)} fusion(s32[1024]{0:T(1024)S(1)} %bitcast.126, f32[4,16,256]{2,1,0:T(8,128)} %collective-permute-done.2, f32[4,16,1024]{2,1,0:T(8,128)S(1)} %get-tuple-element.72, f32[4]{0:T(128)S(1)} %copy-done.12, pred[1024]{0:T(1024)(128)(4,1)S(1)} %get-tuple-element.62, f32[4,96,1024]{2,1,0:T(8,128)S(1)} %convolution_bitcast_fusion), kind=kOutput, calls=%fused_computation.40 | convolution fusion | flops 1008222208 | bytes 857104 | tf_op jit(solution)/shard_map/xiz,zy->xiy/dot_general | solution.py:86
  42.0 0.8 fusion.99
  42.8 0.8 fusion.87
  43.5 0.8 fusion.91
  44.3 0.7 fusion.76
  45.0 0.8 fusion.81
  45.8 48.1 %all-gather.2.cloned.1.call-done = f32[4,4,65536]{2,1,0:T(4,128)} async-done(((f32[1,4,65536]{2,1,0:T(4,128)}), f32[4,4,65536]{2,1,0:T(4,128)}) %all-gather.2.cloned.1.call-update) | async-done | bytes 4194320 | tf_op jit(solution)/shard_map/all_gather | solution.py:202
  93.9 6.1 %dot_general.39 = f32[4,64,1024,4]{2,1,0,3:T(8,128)} reshape(f32[4,65536,4]{1,0,2:T(4,128)} %bitcast.111) | data formatting | bytes 8388608 | tf_op jit(solution)/shard_map/j,jvc->vc/dot_general | solution.py:199
  99.9 0.0 copy-start.2
  99.9 0.0 copy-start.3
  100.0 12.7 %fusion.6 = f32[1,4,64,1024]{3,0,2,1:T(1,128)S(1)} fusion(f32[4,64,1024,4]{2,1,0,3:T(8,128)} %dot_general.39, f32[4,4]{1,0:T(4,128)S(1)} %multiply_subtract_fusion, s32[]{:T(128)S(6)} %select_n.40), kind=kOutput, calls=%fused_computation.6 | convolution fusion | flops 12582912 | bytes 5243396 | tf_op jit(solution)/shard_map/j,jvc->vc/dot_general | solution.py:199
  112.7 0.0 copy-done.2
  112.7 0.0 copy-done.3
  112.7 3.1 %fusion.26 = f32[4,64,1024]{2,1,0:T(8,128)S(1)} fusion(f32[4,96,1024]{2,1,0:T(8,128)} %fusion.81, f32[96,64,1]{0,1,2:T(8,128)S(1)} %copy-done.4, f32[4,64,1024]{2,1,0:T(8,128)S(1)} %copy-done.2, f32[1,64,1024]{2,1,0:T(8,128)S(1)} %get-tuple-element.70, f32[1,64,1024]{2,1,0:T(8,128)S(1)} %copy-done.3, f32[1,64,1024]{2,1,0:T(8,128)S(1)} %get-tuple-element.69, ...), kind=kOutput, calls=%fused_computation.30 | convolution fusion | flops 303562752 | bytes 5791744 | tf_op jit(solution)/shard_map/bc,sbh->sch/dot_general | solution.py:171
  115.8 0.0 copy-start.1
  115.8 1.3 %fusion.60 = f32[1,4,64,1024]{3,2,1,0:T(8,128)} fusion(f32[1,4,64,1024]{3,2,1,0:T(8,128)S(1)} %copy-done, f32[4,64,1024]{2,1,0:T(8,128)S(1)} %fusion.26), kind=kLoop, calls=%fused_computation.46 | loop fusion | flops 524288 | bytes 3145728 | tf_op jit(solution)/shard_map/broadcast_in_dim | solution.py:222
  117.1 0.0 copy-done.1
  (17 shorter events, 0.2 us)
Async XLA Ops:
  7.2 3.1 %copy-start.4 = (f32[96,64,1]{0,1,2:T(8,128)S(1)}, f32[96,64,1]{0,1,2:T(8,128)}, u32[]{:S(2)}) copy-start(f32[96,64,1]{0,1,2:T(8,128)} %constant.191) | copy-start | bytes 73732
  7.2 3.1 %copy-start = (f32[1,4,64,1024]{3,2,1,0:T(8,128)S(1)}, f32[1,4,64,1024]{3,2,1,0:T(8,128)}, u32[]{:S(2)}) copy-start(f32[1,4,64,1024]{3,2,1,0:T(8,128)} %param.21) | copy-start | bytes 3145732
  7.2 86.7 %all-gather.2.cloned.1.call-start = ((), (), s32[]{:S(2)}) async-start(), calls=%async_computation | async-start | bytes 5242880 | tf_op jit(solution)/shard_map/all_gather | solution.py:202
  10.3 11.8 %copy-start.9 = (s32[6,1024]{1,0:T(8,128)S(1)}, s32[6,1024]{1,0:T(8,128)}, u32[]{:S(2)}) copy-start(s32[6,1024]{1,0:T(8,128)} %param.25) | copy-start | bytes 73732
  10.3 11.9 %copy-start.6 = (f32[3,1024]{1,0:T(4,128)S(1)}, f32[3,1024]{1,0:T(4,128)}, u32[]{:S(2)}) copy-start(f32[3,1024]{1,0:T(4,128)} %param.22) | copy-start | bytes 36868
  10.3 11.9 %copy-start.10 = (s32[1,256]{1,0:T(1,128)S(1)}, s32[1,256]{1,0:T(1,128)}, u32[]{:S(2)}) copy-start(s32[1,256]{1,0:T(1,128)} %param.26) | copy-start | bytes 3076
  10.3 11.9 %copy-start.7 = (f32[3,1024]{1,0:T(4,128)S(1)}, f32[3,1024]{1,0:T(4,128)}, u32[]{:S(2)}) copy-start(f32[3,1024]{1,0:T(4,128)} %param.23) | copy-start | bytes 36868
  10.3 11.9 %copy-start.8 = (s32[6,1024]{1,0:T(8,128)S(1)}, s32[6,1024]{1,0:T(8,128)}, u32[]{:S(2)}) copy-start(s32[6,1024]{1,0:T(8,128)} %param.24) | copy-start | bytes 73732
  10.3 12.0 %copy-start.13 = (f32[4]{0:T(128)S(1)}, f32[4]{0:T(128)}, u32[]{:S(2)}) copy-start(f32[4]{0:T(128)} %constant.182.clone.1) | copy-start | bytes 52
  12.4 26.4 %collective-permute-start.2 = (f32[4,16,256]{2,1,0:T(8,128)S(1)}, f32[4,16,256]{2,1,0:T(8,128)}, u32[]{:S(2)}, u32[]{:S(2)}) collective-permute-start(f32[4,16,256]{2,1,0:T(8,128)S(1)} %get-tuple-element.75), channel_id=1, source_target_pairs={{1,0},{3,2},{5,4},{7,6},{9,8},{11,10},{13,12},{15,14},{17,16},{19,... | collective-permute-start | bytes 196616 | tf_op jit(solution)/shard_map/ppermute | solution.py:23
  13.7 22.2 %collective-permute-start.1 = (f32[4,16,256]{2,1,0:T(8,128)}, f32[4,16,256]{2,1,0:T(8,128)}, u32[]{:S(2)}, u32[]{:S(2)}) collective-permute-start(f32[4,16,256]{2,1,0:T(8,128)} %get-tuple-element.76), channel_id=1, source_target_pairs={{0,1},{2,3},{4,5},{6,7},{8,9},{10,11},{12,13},{14,15},{16,17},{18,... | collective-permute-start | bytes 196616 | tf_op jit(solution)/shard_map/ppermute | solution.py:22
  19.8 14.7 %collective-permute-start = (f32[4,16,256]{2,1,0:T(8,128)}, f32[4,16,256]{2,1,0:T(8,128)}, u32[]{:S(2)}, u32[]{:S(2)}) collective-permute-start(f32[4,16,256]{2,1,0:T(8,128)} %get-tuple-element.77), channel_id=1, source_target_pairs={{0,6},{2,0},{4,2},{6,4},{1,7},{3,1},{5,3},{7,5},{8,14},{10,8},{12,... | collective-permute-start | bytes 196616 | tf_op jit(solution)/shard_map/ppermute | solution.py:30
  24.0 1.7 %copy-start.11 = (f32[4]{0:T(128)S(1)}, f32[4]{0:T(128)}, u32[]{:S(2)}) copy-start(f32[4]{0:T(128)} %constant.180.clone.1) | copy-start | bytes 52
  27.4 2.5 %copy-start.5 = (f32[3,64,64,1]{2,1,3,0:T(8,128)S(1)}, f32[3,64,64,1]{2,1,3,0:T(8,128)}, u32[]{:S(2)}) copy-start(f32[3,64,64,1]{2,1,3,0:T(8,128)} %constant.190) | copy-start | bytes 147460
  34.4 1.5 %copy-start.12 = (f32[4]{0:T(128)S(1)}, f32[4]{0:T(128)}, u32[]{:S(2)}) copy-start(f32[4]{0:T(128)} %constant.183.clone.1) | copy-start | bytes 52
  99.9 12.8 %copy-start.2 = (f32[4,64,1024]{2,1,0:T(8,128)S(1)}, f32[4,64,1024]{2,1,0:T(8,128)}, u32[]{:S(2)}) copy-start(f32[4,64,1024]{2,1,0:T(8,128)} %get-tuple-element.102) | copy-start | bytes 3145732
  99.9 12.8 %copy-start.3 = (f32[1,64,1024]{2,1,0:T(8,128)S(1)}, f32[1,64,1024]{2,1,0:T(8,128)}, u32[]{:S(2)}) copy-start(f32[1,64,1024]{2,1,0:T(8,128)} %get-tuple-element.71) | copy-start | bytes 786436
  115.8 1.3 %copy-start.1 = (f32[4,64,1024]{2,1,0:T(8,128)}, f32[4,64,1024]{2,1,0:T(8,128)S(1)}, u32[]{:S(2)}) copy-start(f32[4,64,1024]{2,1,0:T(8,128)S(1)} %fusion.26) | copy-start | bytes 3145732
Sparse Core Ops, SparseCore 0:
  10.4 83.4 all-gather.1
where the time goes:
time: 124 us
  waiting for transfers between devices  48.1 us (39%)
  matrix products  34.9 us (28%)
  between operations  15.1 us (12%)
  local copies, waits for them, and re-layouts  9.9 us (8%)
  starting transfers between devices  8.95 us (7%)
  other arithmetic  7.01 us (6%)
    all_gather x1, waiting for transfers between devices, per_device(): lax.all_gather(flat_state, 'inst', axis=0, tiled=True)  48.1 us
    dot_general x1, matrix products, per_device(): jnp.einsum('j,jvc->vc', inst_row, lax.all_gather(flat_state, 'inst', axis...  12.7 us
    dot_general x6, matrix products, lookup_columns(): jnp.einsum('xiz,zy->xiy', lookup_table, indicator_matrix, precision=maxim...  12.5 us
    ppermute x1, starting transfers between devices, padded_2(): before = lax.ppermute(last, axis, up)  6.09 us
    dot_general x1, local copies, waits for them, and re-layouts, per_device(): jnp.einsum('j,jvc->vc', inst_row, lax.all_gather(flat_state, 'inst', axis...  6.08 us
    unnamed x5, other arithmetic  3.76 us
    dot_general x1, matrix products, body_residual(): jnp.einsum('fga,cat->fcgt', differentiation_tables, state_of_block, preci...  3.74 us
    dot_general x1, matrix products, body_residual(): jnp.einsum('bc,sbh->sch', selector_matrix, lifted_everything, precision=m...  3.09 us
  transfers between devices with their start and end apart: 4, of which 1 were waited for; matrix products, arithmetic and copies ran while one was open for 21% of the time, Pallas kernels for 0%

commit v1 on v0

--- a/solution.py
+++ b/solution.py
@@ -10,6 +10,30 @@
 wave_bound = 1.5
 pseudo_step = 0.05
 maximum_harmonic = lax.Precision.HIGHEST
+
+
+def store_terms(w_in, out_dim, vector):
+    y2 = lax.psum(1, axis_name="inst")
+    placed = lax.axis_index("inst")
+    oldest, seen_now, carry_in = (y2, placed, w_in.shape[out_dim])
+    raw_out = range(oldest)
+    m_next = map(lambda src_i: (src_i, (src_i + 1) % oldest), raw_out)
+    mid_arr = range(oldest)
+    ready = map(lambda src_i: (src_i, (src_i - 1) % oldest), mid_arr)
+    rack = list(ready)
+    heard = oldest // 2
+    met_up = local_part = w_in
+    all_blocks = list(m_next)
+    local_out = vector(w_in, seen_now * carry_in)
+    for tick in range(1, heard + 1):
+        met_up = lax.ppermute(met_up, axis_name="inst", perm=all_blocks)
+        if tick < oldest - heard:
+            local_part = lax.ppermute(local_part, axis_name="inst", perm=rack)
+            out_arr = vector(local_part, (seen_now + tick) % oldest * carry_in)
+            local_out = local_out + out_arr
+        then = vector(met_up, (seen_now - tick) % oldest * carry_in)
+        local_out = local_out + then
+    return local_out
 
 
 def padded_2(value, sides, width):
@@ -196,11 +220,15 @@
     spectral = spectral_matrix(lax.axis_size("inst"))
     flat_state = state_of_block.reshape(1, variables, node_count * elements)
     inst_row = lax.dynamic_index_in_dim(spectral, lax.axis_index("inst"), 0, keepdims=False)
-    spectral_flat = jnp.einsum(
-        "j,jvc->vc",
-        inst_row,
-        lax.all_gather(flat_state, "inst", axis=0, tiled=True),
-        precision=maximum_harmonic,
+    spectral_flat = store_terms(
+        flat_state,
+        0,
+        lambda shard, start: jnp.einsum(
+            "j,jvc->vc",
+            lax.dynamic_slice_in_dim(inst_row, start, shard.shape[0], axis=0),
+            shard,
+            precision=maximum_harmonic,
+        ),
     )
     spectral_term = spectral_flat.reshape(variables, node_count, elements)
     residual = body_residual(

time: 124 us -> 84.8 us (0.68)
  waiting for transfers between devices: 48.1 us -> 28.2 us
  matrix products: 34.9 us -> 21 us
  between operations: 15.1 us -> 2.15 us
  other arithmetic: 7.01 us -> 12.7 us
  starting transfers between devices: 8.95 us -> 12.4 us
  local copies, waits for them, and re-layouts: 9.9 us -> 7.98 us
    all_gather x1 -> x0, waiting for transfers between devices: 48.1 us -> none  [per_device(): lax.all_gather(flat_state, 'inst', axis=0, tiled=True)]
    ppermute x0 -> x3, waiting for transfers between devices: none -> 28.1 us  [the longest x2 22.7 us: store_terms(): met_up = lax.ppermute(met_up, axis_name='inst', perm=all_blocks)]
    dot_general x1 -> x0, matrix products: 12.7 us -> none  [per_device(): jnp.einsum('j,jvc->vc', inst_row, lax.all_gather(flat_state, 'inst', axis...]
    dot_general x1 -> x0, local copies, waits for them, and re-layouts: 6.08 us -> none  [per_device(): jnp.einsum('j,jvc->vc', inst_row, lax.all_gather(flat_state, 'inst', axis...]
    ppermute x0 -> x3, starting transfers between devices: none -> 5.26 us  [the longest x2 3.16 us: store_terms(): met_up = lax.ppermute(met_up, axis_name='inst', perm=all_blocks)]
    add x0 -> x1, other arithmetic: none -> 3.95 us  [store_terms(): local_out = local_out + then]
    unnamed x5 -> x6, other arithmetic: 3.76 us -> 1.69 us
    unnamed x28 -> x75, local copies, waits for them, and re-layouts: 0.08 us -> 2.15 us
  transfers between devices with their start and end apart: 4 -> 6, of which waited for: 1 -> 2; matrix products, arithmetic and copies ran while one was open for 21% -> 37% of each run, Pallas kernels for 0% -> 0%
where the time goes in v1:
time: 84.8 us; the launch traced here: 84.4 us
  waiting for transfers between devices  28.2 us (33%)
  matrix products  21 us (25%)
  other arithmetic  12.7 us (15%)
  starting transfers between devices  12.4 us (15%)
  local copies, waits for them, and re-layouts  7.98 us (9%)
  between operations  2.15 us (3%)
    ppermute x2, waiting for transfers between devices, store_terms(): met_up = lax.ppermute(met_up, axis_name='inst', perm=all_blocks)  22.7 us
    dot_general x6, matrix products, lookup_columns(): jnp.einsum('xiz,zy->xiy', lookup_table, indicator_matrix, precision=maxim...  12.5 us
    ppermute x1, starting transfers between devices, padded_2(): before = lax.ppermute(last, axis, up)  5.77 us
    ppermute x1, waiting for transfers between devices, store_terms(): local_part = lax.ppermute(local_part, axis_name='inst', perm=rack)  5.41 us
    add x1, other arithmetic, store_terms(): local_out = local_out + then  3.95 us
    dot_general x1, matrix products, body_residual(): jnp.einsum('fga,cat->fcgt', differentiation_tables, state_of_block, preci...  3.78 us
    ppermute x2, starting transfers between devices, store_terms(): met_up = lax.ppermute(met_up, axis_name='inst', perm=all_blocks)  3.16 us
    another operation x1, local copies, waits for them, and re-layouts, per_device(): flat_state = state_of_block.reshape(1, variables, node_count * elements)  3 us
  transfers between devices with their start and end apart: 6, of which 2 were waited for; matrix products, arithmetic and copies ran while one was open for 37% of the time, Pallas kernels for 0%

profile of v1, /device:TPU:0, one launch (start us, length us, event | category | flops | bytes accessed | tf_op | source)
XLA Modules:
  0.0 84.4 jit_solution(9165420507817469701)
XLA Ops:
  0.6 0.0 copy-start.16
  0.7 3.0 %reshape_squeeze.3 = f32[1,4,65536]{2,1,0:T(4,128)} reshape(f32[1,4,64,1024]{3,2,1,0:T(8,128)} %param.21) | data formatting | bytes 2097152 | tf_op jit(solution)/shard_map/reshape;squeeze | solution.py:221
  3.7 3.1 %collective-permute-start.1 = (f32[1,4,65536]{2,1,0:T(4,128)}, f32[1,4,65536]{2,1,0:T(4,128)}, u32[]{:S(2)}, u32[]{:S(2)}) collective-permute-start(f32[1,4,65536]{2,1,0:T(4,128)} %reshape_squeeze.3), channel_id=1, source_target_pairs={{0,8},{8,16},{16,24},{24,0},{1,9},{9,17},{17,25},{25,1},{2,10},{10... | collective-permute-start | bytes 3145736 | tf_op jit(solution)/shard_map/ppermute | solution.py:29
  6.8 2.1 %collective-permute-start = (f32[1,4,65536]{2,1,0:T(4,128)}, f32[1,4,65536]{2,1,0:T(4,128)}, u32[]{:S(2)}, u32[]{:S(2)}) collective-permute-start(f32[1,4,65536]{2,1,0:T(4,128)} %reshape_squeeze.3), channel_id=1, source_target_pairs={{0,24},{8,0},{16,8},{24,16},{1,25},{9,1},{17,9},{25,17},{2,26},{10... | collective-permute-start | bytes 3145736 | tf_op jit(solution)/shard_map/ppermute | solution.py:31
  8.9 0.0 copy-done.16
  8.9 1.4 %convolution_bitcast_fusion = f32[4,96,1024]{2,1,0:T(8,128)S(1)} fusion(f32[96,64,1]{0,1,2:T(8,128)S(1)} %copy-done.16, f32[1,4,64,1024]{3,2,1,0:T(8,128)S(1)} %copy-done), kind=kOutput, calls=%fused_computation.26 | convolution fusion | flops 301989888 | bytes 2646016 | tf_op jit(solution)/shard_map/qa,yas->yqs/dot_general | solution.py:209
  10.3 0.0 copy-start.36
  10.3 0.7 fusion.120
  11.0 1.3 %collective-permute-start.5 = (f32[4,16,256]{2,1,0:T(8,128)}, f32[4,16,256]{2,1,0:T(8,128)}, u32[]{:S(2)}, u32[]{:S(2)}) collective-permute-start(f32[4,16,256]{2,1,0:T(8,128)} %get-tuple-element.75), channel_id=1, source_target_pairs={{1,0},{3,2},{5,4},{7,6},{9,8},{11,10},{13,12},{15,14},{17,16},{19,... | collective-permute-start | bytes 196616 | tf_op jit(solution)/shard_map/ppermute | solution.py:47
  12.3 5.8 %collective-permute-start.4 = (f32[4,16,256]{2,1,0:T(8,128)}, f32[4,16,256]{2,1,0:T(8,128)}, u32[]{:S(2)}, u32[]{:S(2)}) collective-permute-start(f32[4,16,256]{2,1,0:T(8,128)} %get-tuple-element.76), channel_id=1, source_target_pairs={{0,1},{2,3},{4,5},{6,7},{8,9},{10,11},{12,13},{14,15},{16,17},{18,... | collective-permute-start | bytes 196616 | tf_op jit(solution)/shard_map/ppermute | solution.py:46
  18.1 0.1 collective-permute-start.3
  18.3 0.6 compare_reduce_fusion
  18.9 0.6 broadcast_multiply_fusion
  19.5 0.6 broadcast_multiply_fusion.1
  20.1 0.6 fusion.124
  20.8 0.7 fusion.126
  21.4 0.7 multiply_bitcast_fusion.1
  22.2 1.6 %fusion.34 = f32[4,16,1024]{2,1,0:T(8,128)S(1)} fusion(s32[1024]{0:T(1024)S(1)} %bitcast.143, f32[4,96,1024]{2,1,0:T(8,128)S(1)} %convolution_bitcast_fusion, f32[4]{0:T(128)S(1)} %copy-done.36, pred[1024]{0:T(1024)(128)(4,1)S(1)} %get-tuple-element.64), kind=kOutput, calls=%fused_computation.32 | convolution fusion | flops 806551552 | bytes 792064 | tf_op jit(solution)/shard_map/xiz,zy->xiy/dot_general | solution.py:110
  23.8 0.0 copy-start.34
  23.9 0.6 slice_multiply_fusion.4
  24.5 0.1 copy-done.10
  24.6 1.6 %fusion.40 = f32[4,16,1024]{2,1,0:T(8,128)S(1)} fusion(s32[1024]{0:T(1024)S(1)} %bitcast.142, f32[4,96,1024]{2,1,0:T(8,128)S(1)} %convolution_bitcast_fusion, f32[4]{0:T(128)S(1)} %copy-done.36, pred[1024]{0:T(1024)(128)(4,1)S(1)} %get-tuple-element.63), kind=kOutput, calls=%fused_computation.34 | convolution fusion | flops 806551552 | bytes 792064 | tf_op jit(solution)/shard_map/xiz,zy->xiy/dot_general | solution.py:110
  26.2 0.0 copy-start.8
  26.2 0.7 fusion.122
  26.9 1.7 %fusion.28 = f32[4,16,1024]{2,1,0:T(8,128)S(1)} fusion(s32[1024]{0:T(1024)S(1)} %bitcast.141, f32[4,96,1024]{2,1,0:T(8,128)S(1)} %convolution_bitcast_fusion, f32[4]{0:T(128)S(1)} %copy-done.34, pred[1024]{0:T(1024)(128)(4,1)S(1)} %get-tuple-element.66), kind=kOutput, calls=%fused_computation.30 | convolution fusion | flops 806551552 | bytes 792064 | tf_op jit(solution)/shard_map/xiz,zy->xiy/dot_general | solution.py:110
  28.6 0.0 copy-done.1
  28.6 0.0 copy-done.8
  28.6 1.6 %fusion.14 = f32[4,16,1024]{2,1,0:T(8,128)S(1)} fusion(s32[1024]{0:T(1024)S(1)} %bitcast.140, f32[4,96,1024]{2,1,0:T(8,128)S(1)} %convolution_bitcast_fusion), kind=kOutput, calls=%fused_computation.16 | convolution fusion | flops 806354944 | bytes 528384 | tf_op jit(solution)/shard_map/xiz,zy->xiy/dot_general | solution.py:110
  30.3 3.8 %multiply_reduce_fusion = (f32[4,64,1024]{2,1,0:T(8,128)}, f32[3,4,64,1024]{3,2,1,0:T(8,128)S(1)}) fusion(f32[3,1024]{1,0:T(4,128)S(1)} %copy-done.19, f32[3,1024]{1,0:T(4,128)S(1)} %copy-done.20, f32[3,64,64,1]{2,1,3,0:T(8,128)S(1)} %copy-done.18, f32[1,4,64,1024]{3,2,1,0:T(8,128)S(1)} %copy-done), kind=kOutput, calls=%fused_computation.19 | convolution fusion | flops 606076928 | bytes 5316608 | tf_op jit(solution)/shard_map/fga,cat->fcgt/dot_general | solution.py:133
  34.1 0.8 fusion.97
  34.9 0.1 slice-done
  35.0 0.8 slice_select_fusion
  35.8 0.8 fusion.92
  36.6 0.0 copy-done.33
  36.6 0.6 broadcast_add_fusion
  37.8 1.6 %copy.12 = f32[1,4,64,1024]{3,1,2,0:T(4,128)} copy(f32[1,4,64,1024]{3,2,1,0:T(8,128)S(1)} %multiply_bitcast_fusion.1) | data formatting | bytes 2097152
  39.4 0.0 collective-permute-done.3
  39.4 1.4 %fusion.58 = f32[4,16,256]{2,1,0:T(8,128)S(1)} fusion(f32[]{:T(128)} %bitcast.121, s32[256]{0:T(256)} %bitcast.145, f32[]{:T(128)S(6)} %sub.84, s32[256]{0:T(256)} %bitcast.144, f32[4,16,256]{2,1,0:T(8,128)} %collective-permute-done.3, f32[4,16,256]{2,1,0:T(8,128)} %get-tuple-element.77), kind=kOutput, calls=%fused_computation.49 | convolution fusion | flops 101351424 | bytes 198664 | tf_op jit(solution)/shard_map/xiz,zy->xiy/dot_general | solution.py:175
  40.8 1.0 %fusion.119 = (f32[4,16,1024]{2,1,0:T(8,128)S(1)}, f32[4,16,1024]{2,1,0:T(8,128)S(1)}, f32[4,16,1024]{2,1,0:T(8,128)S(1)}) fusion(f32[4,96,1024]{2,1,0:T(8,128)S(1)} %copy-done.2, f32[4,16,256]{2,1,0:T(8,128)S(1)} %fusion.58, f32[4,16,768]{2,1,0:T(8,128)} %slice_select_fusion), kind=kLoop, calls=%fused_computation.153 | loop fusion | flops 131072 | bytes 1835008 | tf_op jit(solution)/shard_map/slice | solution.py:212
  41.8 0.0 collective-permute-done.4
  41.9 2.9 %fusion.46 = f32[4,16,1024]{2,1,0:T(8,128)S(1)} fusion(s32[1024]{0:T(1024)S(1)} %bitcast.139, f32[4,16,256]{2,1,0:T(8,128)} %collective-permute-done.4, f32[4,16,1024]{2,1,0:T(8,128)S(1)} %get-tuple-element.74, f32[4]{0:T(128)S(1)} %copy-done.35, pred[1024]{0:T(1024)(128)(4,1)S(1)} %copy-done.32, f32[4,96,1024]{2,1,0:T(8,128)S(1)} %copy-done.2), kind=kOutput, calls=%fused_computation.36 | convolution fusion | flops 1008222208 | bytes 857104 | tf_op jit(solution)/shard_map/xiz,zy->xiy/dot_general | solution.py:110
  44.8 0.0 collective-permute-done.5
  45.0 0.0 copy-done.29
  45.1 0.0 copy-done.31
  45.1 0.0 copy-start.11
  45.1 0.0 copy-start.14
  45.1 0.0 copy-start.15
  45.1 3.1 %fusion.52 = f32[4,16,1024]{2,1,0:T(8,128)S(1)} fusion(s32[1024]{0:T(1024)S(1)} %bitcast.138, f32[4,16,256]{2,1,0:T(8,128)} %collective-permute-done.5, f32[4,16,1024]{2,1,0:T(8,128)S(1)} %get-tuple-element.72, f32[4]{0:T(128)S(1)} %copy-done.35, pred[1024]{0:T(1024)(128)(4,1)S(1)} %copy-done.31, f32[4,96,1024]{2,1,0:T(8,128)S(1)} %copy-done.2), kind=kOutput, calls=%fused_computation.38 | convolution fusion | flops 1008222208 | bytes 857104 | tf_op jit(solution)/shard_map/xiz,zy->xiy/dot_general | solution.py:110
  48.2 0.1 fusion.96
  48.3 0.0 collective-permute-done.1
  48.3 0.1 collective-permute-start.2
  48.4 0.0 copy-start.4
  48.5 0.1 fusion.84
  48.6 0.1 fusion.88
  48.6 0.3 copy-done.27
  48.9 0.1 fusion.73
  48.9 0.1 fusion.78
  49.0 5.4 %collective-permute-done = f32[1,4,65536]{2,1,0:T(4,128)} collective-permute-done((f32[1,4,65536]{2,1,0:T(4,128)}, f32[1,4,65536]{2,1,0:T(4,128)}, u32[]{:S(2)}, u32[]{:S(2)}) %collective-permute-start) | collective-permute-done | bytes 1048608 | tf_op jit(solution)/shard_map/ppermute | solution.py:31
  54.4 22.7 %collective-permute-done.2 = f32[1,4,65536]{2,1,0:T(4,128)S(1)} collective-permute-done((f32[1,4,65536]{2,1,0:T(4,128)}, f32[1,4,65536]{2,1,0:T(4,128)S(1)}, u32[]{:S(2)}, u32[]{:S(2)}) %collective-permute-start.2) | collective-permute-done | bytes 1048608 | tf_op jit(solution)/shard_map/ppermute | solution.py:29
  77.2 4.0 %bitcast_add_fusion.1 = f32[4,65536]{1,0:T(4,128)S(1)} fusion(f32[4,65536]{1,0:T(4,128)S(1)} %bitcast.123, f32[1,4,65536]{2,1,0:T(4,128)S(1)} %collective-permute-done.2, f32[1,4,65536]{2,1,0:T(4,128)} %collective-permute-done.1, f32[1,4,65536]{2,1,0:T(4,128)} %collective-permute-done, f32[]{:T(128)} %bitcast.14, f32[]{:T(128)} %bitcast.12, f32[]{:T(128)} %bitcast.10), kind=kLoop, calls=%fused_computation.41 | loop fusion | flops 1572864 | bytes 5242892 | tf_op jit(solution)/shard_map/add | solution.py:35
  81.1 1.9 %fusion.24 = f32[4,64,1024]{2,1,0:T(8,128)S(1)} fusion(f32[4,96,1024]{2,1,0:T(8,128)S(1)} %fusion.78, f32[96,64,1]{0,1,2:T(8,128)S(1)} %copy-done.17, f32[1,4,64,1024]{3,1,2,0:T(4,128)S(1)} %bitcast.124, f32[4,64,1024]{2,1,0:T(8,128)S(1)} %copy-done.5, f32[1,64,1024]{2,1,0:T(8,128)S(1)} %get-tuple-element.70, f32[1,64,1024]{2,1,0:T(8,128)S(1)} %copy-done.7, ...), kind=kOutput, calls=%fused_computation.28 | convolution fusion | flops 303562752 | bytes 5791744 | tf_op jit(solution)/shard_map/bc,sbh->sch/dot_general | solution.py:195
  83.1 0.0 copy-start.3
  83.1 1.3 %fusion.57 = f32[1,4,64,1024]{3,2,1,0:T(8,128)} fusion(f32[1,4,64,1024]{3,2,1,0:T(8,128)S(1)} %copy-done, f32[4,64,1024]{2,1,0:T(8,128)S(1)} %fusion.24), kind=kLoop, calls=%fused_computation.47 | loop fusion | flops 524288 | bytes 3145728 | tf_op jit(solution)/shard_map/broadcast_in_dim | solution.py:250
  84.4 0.0 copy-done.3
  (67 shorter events, 0.3 us)
Async XLA Ops:
  0.6 8.2 %copy-start.16 = (f32[96,64,1]{0,1,2:T(8,128)S(1)}, f32[96,64,1]{0,1,2:T(8,128)}, u32[]{:S(2)}) copy-start(f32[96,64,1]{0,1,2:T(8,128)} %constant.260) | copy-start | bytes 73732
  0.6 8.2 %copy-start = (f32[1,4,64,1024]{3,2,1,0:T(8,128)S(1)}, f32[1,4,64,1024]{3,2,1,0:T(8,128)}, u32[]{:S(2)}) copy-start(f32[1,4,64,1024]{3,2,1,0:T(8,128)} %param.21) | copy-start | bytes 3145732
  3.6 14.6 %copy-start.26 = (s32[6,1024]{1,0:T(8,128)S(1)}, s32[6,1024]{1,0:T(8,128)}, u32[]{:S(2)}) copy-start(s32[6,1024]{1,0:T(8,128)} %param.25) | copy-start | bytes 73732
  3.7 15.2 %copy-start.19 = (f32[3,1024]{1,0:T(4,128)S(1)}, f32[3,1024]{1,0:T(4,128)}, u32[]{:S(2)}) copy-start(f32[3,1024]{1,0:T(4,128)} %param.22) | copy-start | bytes 36868
  3.7 16.5 %copy-start.20 = (f32[3,1024]{1,0:T(4,128)S(1)}, f32[3,1024]{1,0:T(4,128)}, u32[]{:S(2)}) copy-start(f32[3,1024]{1,0:T(4,128)} %param.23) | copy-start | bytes 36868
  3.7 16.5 %copy-start.25 = (s32[6,1024]{1,0:T(8,128)S(1)}, s32[6,1024]{1,0:T(8,128)}, u32[]{:S(2)}) copy-start(s32[6,1024]{1,0:T(8,128)} %param.24) | copy-start | bytes 73732
  3.7 44.6 %collective-permute-start.1 = (f32[1,4,65536]{2,1,0:T(4,128)}, f32[1,4,65536]{2,1,0:T(4,128)}, u32[]{:S(2)}, u32[]{:S(2)}) collective-permute-start(f32[1,4,65536]{2,1,0:T(4,128)} %reshape_squeeze.3), channel_id=1, source_target_pairs={{0,8},{8,16},{16,24},{24,0},{1,9},{9,17},{17,25},{25,1},{2,10},{10... | collective-permute-start | bytes 3145736 | tf_op jit(solution)/shard_map/ppermute | solution.py:29
  6.8 47.6 %collective-permute-start = (f32[1,4,65536]{2,1,0:T(4,128)}, f32[1,4,65536]{2,1,0:T(4,128)}, u32[]{:S(2)}, u32[]{:S(2)}) collective-permute-start(f32[1,4,65536]{2,1,0:T(4,128)} %reshape_squeeze.3), channel_id=1, source_target_pairs={{0,24},{8,0},{16,8},{24,16},{1,25},{9,1},{17,9},{25,17},{2,26},{10... | collective-permute-start | bytes 3145736 | tf_op jit(solution)/shard_map/ppermute | solution.py:31
  10.3 18.3 %copy-start.1 = (f32[4,96,1024]{2,1,0:T(8,128)}, f32[4,96,1024]{2,1,0:T(8,128)S(1)}, u32[]{:S(2)}) copy-start(f32[4,96,1024]{2,1,0:T(8,128)S(1)} %convolution_bitcast_fusion) | copy-start | bytes 4718596
  10.3 11.8 %copy-start.36 = (f32[4]{0:T(128)S(1)}, f32[4]{0:T(128)}, u32[]{:S(2)}) copy-start(f32[4]{0:T(128)} %constant.251.clone.1) | copy-start | bytes 52
  11.0 33.8 %collective-permute-start.5 = (f32[4,16,256]{2,1,0:T(8,128)}, f32[4,16,256]{2,1,0:T(8,128)}, u32[]{:S(2)}, u32[]{:S(2)}) collective-permute-start(f32[4,16,256]{2,1,0:T(8,128)} %get-tuple-element.75), channel_id=1, source_target_pairs={{1,0},{3,2},{5,4},{7,6},{9,8},{11,10},{13,12},{15,14},{17,16},{19,... | collective-permute-start | bytes 196616 | tf_op jit(solution)/shard_map/ppermute | solution.py:47
  12.3 29.5 %collective-permute-start.4 = (f32[4,16,256]{2,1,0:T(8,128)}, f32[4,16,256]{2,1,0:T(8,128)}, u32[]{:S(2)}, u32[]{:S(2)}) collective-permute-start(f32[4,16,256]{2,1,0:T(8,128)} %get-tuple-element.76), channel_id=1, source_target_pairs={{0,1},{2,3},{4,5},{6,7},{8,9},{10,11},{12,13},{14,15},{16,17},{18,... | collective-permute-start | bytes 196616 | tf_op jit(solution)/shard_map/ppermute | solution.py:46
  18.1 21.4 %collective-permute-start.3 = (f32[4,16,256]{2,1,0:T(8,128)}, f32[4,16,256]{2,1,0:T(8,128)}, u32[]{:S(2)}, u32[]{:S(2)}) collective-permute-start(f32[4,16,256]{2,1,0:T(8,128)} %get-tuple-element.77), channel_id=1, source_target_pairs={{0,6},{2,0},{4,2},{6,4},{1,7},{3,1},{5,3},{7,5},{8,14},{10,8},{12,... | collective-permute-start | bytes 196616 | tf_op jit(solution)/shard_map/ppermute | solution.py:54
  18.9 4.9 %copy-start.21 = (f32[1,1024]{1,0:T(1,128)}, f32[1,1024]{1,0:T(1,128)S(1)}, u32[]{:S(2)}) copy-start(f32[1,1024]{1,0:T(1,128)S(1)} %get-tuple-element.101) | copy-start | bytes 12292
  18.9 4.9 %copy-start.23 = (f32[1,1024]{1,0:T(1,128)}, f32[1,1024]{1,0:T(1,128)S(1)}, u32[]{:S(2)}) copy-start(f32[1,1024]{1,0:T(1,128)S(1)} %get-tuple-element.100) | copy-start | bytes 12292
  23.8 0.7 copy-start.10
  23.8 3.1 %copy-start.34 = (f32[4]{0:T(128)S(1)}, f32[4]{0:T(128)}, u32[]{:S(2)}) copy-start(f32[4]{0:T(128)} %constant.249.clone.1) | copy-start | bytes 52
  26.2 2.4 %copy-start.8 = (f32[4,16,1024]{2,1,0:T(8,128)}, f32[4,16,1024]{2,1,0:T(8,128)S(1)}, u32[]{:S(2)}) copy-start(f32[4,16,1024]{2,1,0:T(8,128)S(1)} %fusion.40) | copy-start | bytes 786436
  26.9 3.4 %copy-start.18 = (f32[3,64,64,1]{2,1,3,0:T(8,128)S(1)}, f32[3,64,64,1]{2,1,3,0:T(8,128)}, u32[]{:S(2)}) copy-start(f32[3,64,64,1]{2,1,3,0:T(8,128)} %constant.259) | copy-start | bytes 147460
  34.1 0.9 %slice-start = ((f32[4,96,1024]{2,1,0:T(8,128)}), f32[4,16,1024]{2,1,0:T(8,128)S(1)}, s32[]{:S(2)}) async-start(f32[4,96,1024]{2,1,0:T(8,128)} %copy-done.1), calls=%async_computation | async-start | bytes 524288 | tf_op jit(solution)/shard_map/slice | solution.py:212
  34.1 2.5 %copy-start.33 = (s32[1,256]{1,0:T(1,128)S(1)}, s32[1,256]{1,0:T(1,128)}, u32[]{:S(2)}) copy-start(s32[1,256]{1,0:T(1,128)} %param.26) | copy-start | bytes 3076
  36.6 4.3 %copy-start.2 = (f32[4,96,1024]{2,1,0:T(8,128)S(1)}, f32[4,96,1024]{2,1,0:T(8,128)}, u32[]{:S(2)}) copy-start(f32[4,96,1024]{2,1,0:T(8,128)} %copy-done.1) | copy-start | bytes 4718596
  39.4 2.4 %copy-start.30 = (s32[1,1024]{1,0:T(1,128)S(1)}, s32[1,1024]{1,0:T(1,128)}, u32[]{:S(2)}) copy-start(s32[1,1024]{1,0:T(1,128)} %get-tuple-element.95) | copy-start | bytes 12292
  39.4 2.4 %copy-start.32 = (pred[1024]{0:T(1024)(128)(4,1)S(1)}, pred[1024]{0:T(1024)(128)(4,1)}, u32[]{:S(2)}) copy-start(pred[1024]{0:T(1024)(128)(4,1)} %get-tuple-element.67) | copy-start | bytes 3076
  39.4 2.4 %copy-start.35 = (f32[4]{0:T(128)S(1)}, f32[4]{0:T(128)}, u32[]{:S(2)}) copy-start(f32[4]{0:T(128)} %constant.252.clone.1) | copy-start | bytes 52
  41.8 3.2 %copy-start.29 = (s32[1,1024]{1,0:T(1,128)S(1)}, s32[1,1024]{1,0:T(1,128)}, u32[]{:S(2)}) copy-start(s32[1,1024]{1,0:T(1,128)} %get-tuple-element.90) | copy-start | bytes 12292
  41.8 3.2 %copy-start.31 = (pred[1024]{0:T(1024)(128)(4,1)S(1)}, pred[1024]{0:T(1024)(128)(4,1)}, u32[]{:S(2)}) copy-start(pred[1024]{0:T(1024)(128)(4,1)} %get-tuple-element.62) | copy-start | bytes 3076
  44.8 3.5 %copy-start.6 = (f32[4,96,1024]{2,1,0:T(8,128)S(1)}, f32[4,96,1024]{2,1,0:T(8,128)}, u32[]{:S(2)}) copy-start(f32[4,96,1024]{2,1,0:T(8,128)} %fusion.92) | copy-start | bytes 4718596
  44.8 3.5 %copy-start.24 = (f32[1,1024]{1,0:T(1,128)S(1)}, f32[1,1024]{1,0:T(1,128)}, u32[]{:S(2)}) copy-start(f32[1,1024]{1,0:T(1,128)} %copy-done.23) | copy-start | bytes 12292
  45.1 3.4 %copy-start.11 = (f32[4,16,1024]{2,1,0:T(8,128)S(1)}, f32[4,16,1024]{2,1,0:T(8,128)}, u32[]{:S(2)}) copy-start(f32[4,16,1024]{2,1,0:T(8,128)} %copy-done.10) | copy-start | bytes 786436
  45.1 3.4 %copy-start.14 = (f32[1,16,1024]{2,1,0:T(8,128)S(1)}, f32[1,16,1024]{2,1,0:T(8,128)}, u32[]{:S(2)}) copy-start(f32[1,16,1024]{2,1,0:T(8,128)} %get-tuple-element.84) | copy-start | bytes 196612
  45.1 3.4 %copy-start.15 = (f32[1,16,1024]{2,1,0:T(8,128)S(1)}, f32[1,16,1024]{2,1,0:T(8,128)}, u32[]{:S(2)}) copy-start(f32[1,16,1024]{2,1,0:T(8,128)} %get-tuple-element.85) | copy-start | bytes 196612
  45.1 3.4 %copy-start.28 = (f32[1024]{0:T(1024)S(1)}, f32[1024]{0:T(1024)}, u32[]{:S(2)}) copy-start(f32[1024]{0:T(1024)} %broadcast_multiply_fusion.1) | copy-start | bytes 12292
  45.1 3.4 %copy-start.9 = (f32[4,16,1024]{2,1,0:T(8,128)S(1)}, f32[4,16,1024]{2,1,0:T(8,128)}, u32[]{:S(2)}) copy-start(f32[4,16,1024]{2,1,0:T(8,128)} %copy-done.8) | copy-start | bytes 786436
  45.1 3.4 %copy-start.12 = (f32[1,16,1024]{2,1,0:T(8,128)S(1)}, f32[1,16,1024]{2,1,0:T(8,128)}, u32[]{:S(2)}) copy-start(f32[1,16,1024]{2,1,0:T(8,128)} %get-tuple-element.82) | copy-start | bytes 196612
  45.1 3.4 %copy-start.13 = (f32[1,16,1024]{2,1,0:T(8,128)S(1)}, f32[1,16,1024]{2,1,0:T(8,128)}, u32[]{:S(2)}) copy-start(f32[1,16,1024]{2,1,0:T(8,128)} %get-tuple-element.83) | copy-start | bytes 196612
  45.1 3.4 %copy-start.22 = (f32[1,1024]{1,0:T(1,128)S(1)}, f32[1,1024]{1,0:T(1,128)}, u32[]{:S(2)}) copy-start(f32[1,1024]{1,0:T(1,128)} %copy-done.21) | copy-start | bytes 12292
  48.2 0.7 copy-start.27
  48.3 28.8 %collective-permute-start.2 = (f32[1,4,65536]{2,1,0:T(4,128)}, f32[1,4,65536]{2,1,0:T(4,128)S(1)}, u32[]{:S(2)}, u32[]{:S(2)}) collective-permute-start(f32[1,4,65536]{2,1,0:T(4,128)} %collective-permute-done.1), channel_id=1, source_target_pairs={{0,8},{8,16},{16,24},{24,0},{1,9},{9,17},{17,25},{25,1},{2,10},{10... | collective-permute-start | bytes 3145736 | tf_op jit(solution)/shard_map/ppermute | solution.py:29
  48.4 28.7 %copy-start.4 = (f32[1,4,64,1024]{3,1,2,0:T(4,128)S(1)}, f32[1,4,64,1024]{3,1,2,0:T(4,128)}, u32[]{:S(2)}) copy-start(f32[1,4,64,1024]{3,1,2,0:T(4,128)} %copy.12) | copy-start | bytes 3145732
  77.1 4.0 %copy-start.5 = (f32[4,64,1024]{2,1,0:T(8,128)S(1)}, f32[4,64,1024]{2,1,0:T(8,128)}, u32[]{:S(2)}) copy-start(f32[4,64,1024]{2,1,0:T(8,128)} %get-tuple-element.106) | copy-start | bytes 3145732
  77.2 4.0 %copy-start.7 = (f32[1,64,1024]{2,1,0:T(8,128)S(1)}, f32[1,64,1024]{2,1,0:T(8,128)}, u32[]{:S(2)}) copy-start(f32[1,64,1024]{2,1,0:T(8,128)} %get-tuple-element.71) | copy-start | bytes 786436
  77.2 4.0 %copy-start.17 = (f32[96,64,1]{0,1,2:T(8,128)S(1)}, f32[96,64,1]{0,1,2:T(8,128)}, u32[]{:S(2)}) copy-start(f32[96,64,1]{0,1,2:T(8,128)} %constant.260) | copy-start | bytes 73732
  83.1 1.3 %copy-start.3 = (f32[4,64,1024]{2,1,0:T(8,128)}, f32[4,64,1024]{2,1,0:T(8,128)S(1)}, u32[]{:S(2)}) copy-start(f32[4,64,1024]{2,1,0:T(8,128)S(1)} %fusion.24) | copy-start | bytes 3145732
